TPU v7x, 32 devices: a whole 2x2x4 slice. The times are simulated.
32 devices in a mesh: grp: 4 (over x, core), seq: 8 (over z, y).
Axes of the slice: x: 2, y: 2, z: 4, core: 2. Of those that a mesh axis runs over, the one named last changes fastest.
Arguments:
- signal: float32 [64, 2048, 768], P('grp', 'seq'), may hold values from -36 to 36
- entry_gain: float32 [768], replicated
- entry_shift: float32 [768], replicated, may hold values from -3 to 3
- dilated_kernel: float32 [3, 768, 384], replicated
- middle_gain: float32 [384], replicated
- middle_shift: float32 [384], replicated, may hold values from -3 to 3
- pointwise_kernel: float32 [384, 768], replicated
- pointwise_bias: float32 [768], replicated, may hold values from -3 to 3
- lengths: int32 [64], replicated, may hold values from 128 to 1024, as said below
- assignment: int32 [4, 16], P('grp'), may hold values from 0 to 15, as said below
- cotangent: float32 [65536, 768], P(('grp', 'seq')), may hold values from -6 to 6
Outputs:
- activations: float32 [65536, 768], P(('grp', 'seq'))
- signal_gradient: float32 [64, 2048, 768], P('grp', 'seq')
- entry_gain_gradient: float32 [768], replicated
- entry_shift_gradient: float32 [768], replicated
- dilated_kernel_gradient: float32 [3, 768, 384], replicated
- middle_gain_gradient: float32 [384], replicated
- middle_shift_gradient: float32 [384], replicated
- pointwise_kernel_gradient: float32 [384, 768], replicated
- pointwise_bias_gradient: float32 [768], replicated
Inputs may be any that keep to these rules, and one draw needn't show every extreme that they name: `lengths`: valid rows of a window come first; some window is full with 1024 rows and some has exactly 128. `assignment`: each row lists the 16 windows of one group once.
All inputs are finite; a program needn't handle non-finite values.
Results may differ from a plain program's by a relative error of at most 0.0066.
Values may be sent and summed in bfloat16 or wider, within the bound.
No kernel may reach another device: no remote copies, remote signals or barrier semaphores. Data moves between devices by JAX's collectives and lax.ppermute only.
A program may use at most 128 MiB of HBM per device.

v0:
```python
import jax
import jax.numpy as jnp
from jax import lax
from jax.sharding import PartitionSpec as P

DILATION_STEP = 38
WINDOW_SPAN = 1024
HALF_WINDOW_ROWS = 512
EPSILON = 0.001


def from_partner(block, axis, bit):
    count = lax.axis_size(axis)
    route = []
    for low in range(count):
        high = low | 1 << bit
        if high != low and high < count:
            route += [(low, high), (high, low)]
    return lax.ppermute(block, axis, route)


def smooth(values):
    return jax.nn.gelu(values, approximate=True)


def moments(values, valid_mask, row_count):
    centre = lax.psum(jnp.sum(values * valid_mask, axis=(0, 1)), ("grp", "seq")) / row_count
    deviation = (values - centre) * valid_mask
    spread = lax.psum(jnp.sum(deviation * deviation, axis=(0, 1)), ("grp", "seq")) / row_count
    return (centre, lax.rsqrt(spread + EPSILON))


def extended(resident_rows, neighbour_border):
    position_count = resident_rows.shape[0]
    channel_width = resident_rows.shape[2]
    empty_row_block = jnp.zeros((position_count, DILATION_STEP, channel_width), resident_rows.dtype)
    bottom_portion = jnp.concatenate(
        [empty_row_block, resident_rows[:, :HALF_WINDOW_ROWS], neighbour_border[:, DILATION_STEP:]],
        axis=1,
    )
    top_portion = jnp.concatenate(
        [neighbour_border[:, :DILATION_STEP], resident_rows[:, HALF_WINDOW_ROWS:], empty_row_block],
        axis=1,
    )
    return jnp.stack([bottom_portion, top_portion], axis=1).reshape(
        2 * position_count, HALF_WINDOW_ROWS + 2 * DILATION_STEP, channel_width
    )


def per_device(
    signal,
    entry_gain,
    entry_shift,
    dilated_kernel,
    middle_gain,
    middle_shift,
    pointwise_kernel,
    pointwise_bias,
    lengths,
    assignment,
    cotangent,
):
    seq_count = lax.axis_size("seq")
    seq_place = lax.axis_index("seq")
    grp_place = lax.axis_index("grp")
    group_windows, segment, channel_width = signal.shape
    source_rows = segment // 2
    position_count = group_windows // seq_count
    bin_pairs = signal.reshape(group_windows, source_rows, 2, channel_width)
    first_bin = bin_pairs[:, :, 0]
    second_bin = bin_pairs[:, :, 1]
    take_first = first_bin >= second_bin
    group_lengths = lax.dynamic_slice_in_dim(lengths, grp_place * group_windows, group_windows)
    source_position = seq_place * source_rows + jnp.arange(source_rows, dtype=jnp.int32)
    source_valid = (source_position[None, :] < group_lengths[:, None]).astype(jnp.float32)[
        :, :, None
    ]
    pooled_low = (jnp.where(take_first, first_bin, second_bin) * source_valid).astype(jnp.bfloat16)
    window_order = assignment[0]
    upper_source = (seq_place >= seq_count // 2).astype(jnp.int32)
    targets = jnp.arange(seq_count, dtype=jnp.int32)
    slot_range = jnp.arange(position_count, dtype=jnp.int32)
    picked = window_order[
        (
            jnp.bitwise_xor(targets, upper_source)[:, None] * position_count + slot_range[None, :]
        ).reshape(-1)
    ]
    outgoing = jnp.take(pooled_low, picked, axis=0)
    arrived = lax.all_to_all(outgoing, "seq", split_axis=0, concat_axis=1, tiled=True)
    partner_place = jnp.bitwise_xor(seq_place, 1)
    own_windows = lax.dynamic_slice_in_dim(window_order, seq_place * position_count, position_count)
    partner_windows = lax.dynamic_slice_in_dim(
        window_order, partner_place * position_count, position_count
    )
    row_position = jnp.arange(WINDOW_SPAN, dtype=jnp.int32)
    limit_rows = jnp.where(
        row_position[None, :] < HALF_WINDOW_ROWS,
        jnp.take(group_lengths, own_windows)[:, None],
        jnp.take(group_lengths, partner_windows)[:, None],
    )
    valid_mask = (row_position[None, :] < limit_rows).astype(jnp.float32)[:, :, None]
    row_count = jnp.sum(lengths.astype(jnp.float32))
    pooled = arrived.astype(jnp.float32)
    entry_centre, entry_scale = moments(pooled, valid_mask, row_count)
    entry_norm = (pooled - entry_centre) * entry_scale
    entry_smooth, entry_back = jax.vjp(smooth, entry_norm * entry_gain + entry_shift)
    entry_activation = (entry_smooth * valid_mask).astype(jnp.bfloat16)
    kernel_low = dilated_kernel.astype(jnp.bfloat16)
    entry_border = from_partner(
        entry_activation[:, HALF_WINDOW_ROWS - DILATION_STEP : HALF_WINDOW_ROWS + DILATION_STEP],
        "seq",
        0,
    )
    entry_widened = extended(entry_activation, entry_border)
    dilated_out = jnp.zeros(
        (2 * position_count, HALF_WINDOW_ROWS, kernel_low.shape[2]), jnp.float32
    )
    for kernel_tap_index in range(3):
        displaced_rows = entry_widened[
            :,
            kernel_tap_index * DILATION_STEP : kernel_tap_index * DILATION_STEP + HALF_WINDOW_ROWS,
        ]
        dilated_out = dilated_out + jnp.einsum(
            "hrc,cf->hrf",
            displaced_rows,
            kernel_low[kernel_tap_index],
            preferred_element_type=jnp.float32,
        )
    dilated_out = dilated_out.reshape(position_count, WINDOW_SPAN, -1)
    middle_centre, middle_scale = moments(dilated_out, valid_mask, row_count)
    middle_norm = (dilated_out - middle_centre) * middle_scale
    middle_smooth, middle_back = jax.vjp(smooth, middle_norm * middle_gain + middle_shift)
    middle_act = (middle_smooth * valid_mask).astype(jnp.bfloat16)
    pointwise_low = pointwise_kernel.astype(jnp.bfloat16)
    mixed_out = jnp.einsum(
        "krf,fd->krd", middle_act, pointwise_low, preferred_element_type=jnp.float32
    )
    activations = (valid_mask * (pooled + mixed_out + pointwise_bias)).reshape(-1, channel_width)
    grad_block = cotangent.reshape(position_count, WINDOW_SPAN, channel_width) * valid_mask
    grad_mixed = grad_block.astype(jnp.bfloat16)
    bias_part = jnp.sum(grad_block, axis=(0, 1))
    pointwise_part = jnp.einsum(
        "krf,krd->fd", middle_act, grad_mixed, preferred_element_type=jnp.float32
    )
    grad_middle = jnp.einsum(
        "krd,fd->krf", grad_mixed, pointwise_low, preferred_element_type=jnp.float32
    )
    grad_middle_pre = middle_back(grad_middle * valid_mask)[0]
    middle_gain_part = jnp.sum(grad_middle_pre * middle_norm, axis=(0, 1))
    middle_shift_part = jnp.sum(grad_middle_pre, axis=(0, 1))
    (
        middle_gain_gradient,
        middle_shift_gradient,
        pointwise_kernel_gradient,
        pointwise_bias_gradient,
    ) = lax.psum((middle_gain_part, middle_shift_part, pointwise_part, bias_part), ("grp", "seq"))
    dilated_gradient = (
        middle_gain
        * middle_scale
        * (
            grad_middle_pre
            - (middle_shift_gradient + middle_norm * middle_gain_gradient) / row_count
        )
        * valid_mask
    )
    dilated_gradient = dilated_gradient.astype(jnp.bfloat16)
    border_gradient = from_partner(
        dilated_gradient[:, HALF_WINDOW_ROWS - DILATION_STEP : HALF_WINDOW_ROWS + DILATION_STEP],
        "seq",
        0,
    )
    grad_wide = extended(dilated_gradient, border_gradient)
    grad_halves = dilated_gradient.reshape(2 * position_count, HALF_WINDOW_ROWS, -1)
    kernel_pieces = []
    grad_entry = jnp.zeros((2 * position_count, HALF_WINDOW_ROWS, channel_width), jnp.float32)
    for kernel_tap_index in range(3):
        displaced_rows = entry_widened[
            :,
            kernel_tap_index * DILATION_STEP : kernel_tap_index * DILATION_STEP + HALF_WINDOW_ROWS,
        ]
        kernel_pieces.append(
            jnp.einsum(
                "hrc,hrf->cf", displaced_rows, grad_halves, preferred_element_type=jnp.float32
            )
        )
        backward_offset = (2 - kernel_tap_index) * DILATION_STEP
        grad_shifted = grad_wide[:, backward_offset : backward_offset + HALF_WINDOW_ROWS]
        grad_entry = grad_entry + jnp.einsum(
            "hrf,cf->hrc",
            grad_shifted,
            kernel_low[kernel_tap_index],
            preferred_element_type=jnp.float32,
        )
    kernel_part = jnp.stack(kernel_pieces)
    grad_entry = grad_entry.reshape(position_count, WINDOW_SPAN, channel_width)
    grad_entry_pre = entry_back(grad_entry * valid_mask)[0]
    entry_gain_part = jnp.sum(grad_entry_pre * entry_norm, axis=(0, 1))
    entry_shift_part = jnp.sum(grad_entry_pre, axis=(0, 1))
    entry_gain_gradient, entry_shift_gradient, dilated_kernel_gradient = lax.psum(
        (entry_gain_part, entry_shift_part, kernel_part), ("grp", "seq")
    )
    grad_pooled = (
        entry_gain
        * entry_scale
        * (grad_entry_pre - (entry_shift_gradient + entry_norm * entry_gain_gradient) / row_count)
        * valid_mask
        + grad_block
    )
    returned = lax.all_to_all(
        grad_pooled.astype(jnp.bfloat16), "seq", split_axis=1, concat_axis=0, tiled=True
    )
    inverse = (
        jnp.zeros((group_windows,), jnp.int32)
        .at[picked]
        .set(jnp.arange(group_windows, dtype=jnp.int32))
    )
    grad_source = jnp.take(returned, inverse, axis=0).astype(jnp.float32) * source_valid
    zero_part = jnp.zeros_like(grad_source)
    signal_gradient = jnp.stack(
        [
            jnp.where(take_first, grad_source, zero_part),
            jnp.where(take_first, zero_part, grad_source),
        ],
        axis=2,
    ).reshape(group_windows, segment, channel_width)
    return (
        activations,
        signal_gradient,
        entry_gain_gradient,
        entry_shift_gradient,
        dilated_kernel_gradient,
        middle_gain_gradient,
        middle_shift_gradient,
        pointwise_kernel_gradient,
        pointwise_bias_gradient,
    )


def solution(mesh):
    return jax.shard_map(
        per_device,
        mesh=mesh,
        in_specs=(
            P("grp", "seq", None),
            P(),
            P(),
            P(),
            P(),
            P(),
            P(),
            P(),
            P(),
            P("grp", None),
            P(("grp", "seq"), None),
        ),
        out_specs=(
            P(("grp", "seq"), None),
            P("grp", "seq", None),
            P(),
            P(),
            P(),
            P(),
            P(),
            P(),
            P(),
        ),
        check_vma=False,
    )
```

profile of v0, /device:TPU:0, one launch (start us, length us, event | category | flops | bytes accessed | tf_op | source)
XLA Modules:
  0.0 660.3 jit_solution(9878125855591612174)
XLA Ops:
  8.7 16.6 %copy.79 = f32[16,256,768]{2,0,1:T(8,128)} copy(f32[16,256,768]{2,1,0:T(8,128)} %param.15) | data formatting | bytes 25165824 | tf_op args[0]
  25.4 10.5 %fusion.86 = (f32[16,128,1,768]{3,0,2,1:T(8,128)}, f32[16,128,1,768]{3,0,2,1:T(8,128)}) fusion(f32[16,128,2,768]{3,0,2,1:T(8,128)} %bitcast.168), kind=kLoop, calls=%fused_computation.166 | loop fusion | bytes 25165824 | tf_op jit(solution)/shard_map/slice | solution.py:71
  36.1 11.7 %multiply_convert_fusion.1 = (bf16[16,128,768]{2,1,0:T(8,128)(2,1)}, pred[16,128,768]{2,1,0:T(8,128)(4,1)}) fusion(f32[16,128,1,768]{3,0,2,1:T(8,128)} %get-tuple-element.66, f32[16,128,1,768]{3,0,2,1:T(8,128)} %get-tuple-element.65, f32[16,128]{1,0:T(8,128)S(1)} %compare_convert_fusion.2), kind=kLoop, calls=%fused_computation.48 | loop fusion | flops 6291456 | bytes 17309696 | tf_op jit(solution)/shard_map/convert_element_type | solution.py:78
  47.8 2.6 gather_fusion.3
  50.4 2.0 broadcast_select_fusion.1
  52.4 7.4 %all-to-all-start = ((bf16[16,128,768]{2,1,0:T(8,128)(2,1)}), bf16[16,128,768]{2,1,0:T(8,128)(2,1)S(1)}, u32[]{:S(2)}, u32[]{:S(2)}) async-start(bf16[16,128,768]{2,1,0:T(8,128)(2,1)} %broadcast_select_fusion.1), calls=%async_computation | async-start | bytes 6291456 | tf_op jit(solution)/shard_map/all_to_all | solution.py:89
  61.7 3.7 convert_element_type.105
  66.3 5.2 multiply_convert_fusion.2
  71.5 3.5 fusion.38
  75.1 55.5 %all-to-all-done = bf16[16,128,768]{2,1,0:T(8,128)(2,1)S(1)} async-done(((bf16[16,128,768]{2,1,0:T(8,128)(2,1)}), bf16[16,128,768]{2,1,0:T(8,128)(2,1)S(1)}, u32[]{:S(2)}, u32[]{:S(2)}) %all-to-all-start) | async-done | bytes 3145760 | tf_op jit(solution)/shard_map/all_to_all | solution.py:89
  131.3 37.8 %psum.77 = f32[768]{0:T(1024)S(1)} all-reduce(f32[768]{0:T(1024)S(1)} %multiply_reduce_fusion.2), channel_id=1, replica_groups=mesh['grp'=4,'seq'=8] {'grp','seq'}, use_global_device_ids=true, to_apply=%region_1.4 | all-reduce | flops 768 | bytes 6144 | tf_op jit(solution)/shard_map/psum | solution.py:27
  170.8 41.7 %psum.78 = f32[768]{0:T(1024)S(1)} all-reduce(f32[768]{0:T(1024)S(1)} %multiply_reduce_fusion.1), channel_id=1, replica_groups=mesh['grp'=4,'seq'=8] {'grp','seq'}, use_global_device_ids=true, to_apply=%region_4.7 | all-reduce | flops 768 | bytes 6144 | tf_op jit(solution)/shard_map/psum | solution.py:29
  214.6 3.4 multiply_convert_fusion
  218.1 2.3 collective-permute-start
  220.6 4.9 collective-permute-done
  227.3 1.9 copy-done.10
  229.2 1.8 fusion.43
  231.0 1.8 fusion.51
  232.9 2.0 multiply_reduce_fusion.6
  234.9 38.2 %psum.79 = f32[384]{0:T(512)S(1)} all-reduce(f32[384]{0:T(512)S(1)} %get-tuple-element.86), channel_id=1, replica_groups=mesh['grp'=4,'seq'=8] {'grp','seq'}, use_global_device_ids=true, to_apply=%region_6.9 | all-reduce | flops 384 | bytes 3072 | tf_op jit(solution)/shard_map/psum | solution.py:27
  274.2 41.7 %psum.80 = f32[384]{0:T(512)S(1)} all-reduce(f32[384]{0:T(512)S(1)} %multiply_reduce_fusion.5), channel_id=1, replica_groups=mesh['grp'=4,'seq'=8] {'grp','seq'}, use_global_device_ids=true, to_apply=%region_8.11 | all-reduce | flops 384 | bytes 3072 | tf_op jit(solution)/shard_map/psum | solution.py:29
  316.6 6.1 fusion.81
  322.7 38.7 %all-reduce.1 = (f32[384]{0:T(512)S(1)}, f32[384]{0:T(512)S(1)}) all-reduce(f32[384]{0:T(512)S(1)} %get-tuple-element.50, f32[384]{0:T(512)S(1)} %get-tuple-element.49), channel_id=1, replica_groups=mesh['grp'=4,'seq'=8] {'grp','seq'}, use_global_device_ids=true, to_apply=%region_12.15 | all-reduce | flops 768 | bytes 6144 | tf_op jit(solution)/shard_map/psum | solution.py:156
  361.4 3.0 multiply_convert_fusion.5
  364.5 2.3 collective-permute-start.1
  367.0 2.7 collective-permute-done.1
  371.6 1.8 fusion.56
  373.5 1.8 fusion.58
  375.3 8.2 %fusion.80 = (f32[768]{0:T(1024)S(1)}, f32[768]{0:T(1024)S(1)}, f32[4,512,768]{2,1,0:T(8,128)}) fusion(f32[768]{0:T(1024)S(1)} %get-tuple-element.59, f32[4,512,768]{2,1,0:T(8,128)S(1)} %bitcast.163, f32[768]{0:T(1024)S(1)} %broadcast_divide_fusion, f32[768]{0:T(1024)S(1)} %copy-done.15, f32[768]{0:T(1024)S(1)} %copy-done.13, f32[4,512]{1,0:T(4,128)S(1)} %fusion.74, ...), kind=kOutput, calls=%fused_computation.162 | convolution fusion | flops 1253571072 | bytes 27359232 | tf_op jit(solution)/shard_map/hrf,cf->hrc/dot_general | solution.py:188
  383.5 41.3 %all-reduce = (f32[768]{0:T(1024)S(1)}, f32[768]{0:T(1024)S(1)}, f32[768]{0:T(1024)}) all-reduce(f32[768]{0:T(1024)S(1)} %get-tuple-element.48, f32[768]{0:T(1024)S(1)} %get-tuple-element.47, f32[768]{0:T(1024)S(1)} %get-tuple-element.68), channel_id=1, replica_groups=mesh['grp'=4,'seq'=8] {'grp','seq'}, use_global_device_ids=true, to_apply=%region_16.19 | all-reduce | flops 2304 | bytes 18432 | tf_op jit(solution)/shard_map/psum | solution.py:199
  424.8 11.1 %fusion.10 = bf16[2,1024,768]{2,1,0:T(8,128)(2,1)S(1)} fusion(f32[2,1024,768]{2,1,0:T(8,128)} %bitcast.164, f32[2,8,128,768]{3,2,1,0:T(8,128)} %copy-done.1, f32[]{:T(128)} %convert_reduce_fusion, f32[768]{0:T(1024)S(1)} %get-tuple-element.95, f32[768]{0:T(1024)S(1)} %get-tuple-element.96, f32[768]{0:T(1024)S(1)} %get-tuple-element.58, ...), kind=kLoop, calls=%fused_computation.21 | loop fusion | flops 51904512 | bytes 22049796 | tf_op jit(solution)/shard_map/convert_element_type | solution.py:210
  435.9 5.0 copy.86
  440.9 5.2 all-to-all-start.1
  446.2 4.3 fusion.60
  450.5 1.8 fusion.66
  452.3 1.8 fusion.63
  454.2 2.0 pad_maximum_fusion.2
  458.1 2.4 convolution_bitcast_fusion
  462.3 7.3 %fusion.19 = f32[2,1024,768]{2,1,0:T(8,128)} fusion(f32[2,8,128,768]{3,2,1,0:T(8,128)} %copy-done.1, f32[768]{0:T(1024)S(1)} %copy-done.17, f32[2,1024]{1,0:T(2,128)S(1)} %compare_convert_fusion.1, bf16[2,1024,384]{2,1,0:T(8,128)(2,1)S(1)} %copy-done.5, f32[384,768]{1,0:T(8,128)S(1)} %copy-done.7), kind=kOutput, calls=%fused_computation.36 | convolution fusion | flops 1212973056 | bytes 15346688 | tf_op jit(solution)/shard_map/krf,fd->krd/dot_general | solution.py:135
  469.6 68.6 %all-to-all-done.1 = bf16[2,1024,768]{2,0,1:T(2,128)(2,1)} async-done(((bf16[2,1024,768]{2,0,1:T(2,128)(2,1)}), bf16[2,1024,768]{2,0,1:T(2,128)(2,1)}, u32[]{:S(2)}, u32[]{:S(2)}) %all-to-all-start.1) | async-done | bytes 3145760 | tf_op jit(solution)/shard_map/all_to_all | solution.py:209
  538.2 2.3 copy.87
  540.7 2.4 gather_fusion.4
  543.1 5.3 select_bitcast_fusion.1
  548.4 9.2 %pad_maximum_fusion = f32[16,128,2,768]{3,1,0,2:T(8,128)} fusion(f32[16,128,1,768]{3,1,0,2:T(8,128)} %get-tuple-element.70, f32[16,128,1,768]{3,1,0,2:T(8,128)S(1)} %get-tuple-element.69), kind=kLoop, calls=%fused_computation.6 | loop fusion | flops 3145728 | bytes 25165824 | tf_op jit(solution)/shard_map/stack | solution.py:219
  557.6 16.5 %copy.89 = f32[16,128,2,768]{3,0,2,1:T(8,128)} copy(f32[16,128,2,768]{3,1,0,2:T(8,128)} %pad_maximum_fusion) | data formatting | bytes 25165824 | tf_op jit(solution)/shard_map/stack | solution.py:219
  574.0 16.9 %copy.94 = f32[16,256,768]{2,1,0:T(8,128)} copy(f32[16,256,768]{2,0,1:T(8,128)} %bitcast.169) | data formatting | bytes 25165824
  590.9 57.0 %all-reduce.5.cloned.1.call-done = (f32[3,768,384]{2,1,0:T(8,128)}, f32[384,768]{1,0:T(8,128)}) async-done(((f32[3,768,384]{2,1,0:T(8,128)}, f32[384,768]{1,0:T(8,128)}), (f32[3,768,384]{2,1,0:T(8,128)}, f32[384,768]{1,0:T(8,128)})) %all-reduce.5.cloned.1.call-update) | async-done | bytes 4718608 | tf_op jit(solution)/shard_map/psum | solution.py:199
  647.9 4.1 copy.127
  (128 shorter events, 19.6 us)
Async XLA Ops:
  25.4 10.5 %copy-start.22 = (s32[64]{0:T(128)S(1)}, s32[64]{0:T(128)}, u32[]{:S(2)}) copy-start(s32[64]{0:T(128)} %param.23) | copy-start | bytes 772
  52.4 7.5 %copy-start = (s32[1,16]{1,0:T(1,128)S(1)}, s32[1,16]{1,0:T(1,128)}, u32[]{:S(2)}) copy-start(s32[1,16]{1,0:T(1,128)} %param.24) | copy-start | bytes 196
  52.4 78.1 %all-to-all-start = ((bf16[16,128,768]{2,1,0:T(8,128)(2,1)}), bf16[16,128,768]{2,1,0:T(8,128)(2,1)S(1)}, u32[]{:S(2)}, u32[]{:S(2)}) async-start(bf16[16,128,768]{2,1,0:T(8,128)(2,1)} %broadcast_select_fusion.1), calls=%async_computation | async-start | bytes 6291456 | tf_op jit(solution)/shard_map/all_to_all | solution.py:89
  61.7 9.9 %slice-start.2 = ((s8[6291456]{0:T(1024)(128)(4,1)}), s8[4194304]{0:T(1024)(128)(4,1)S(1)}, s32[]{:S(2)}) async-start(s8[6291456]{0:T(1024)(128)(4,1)} %bitcast.165), calls=%async_computation.5 | async-start | bytes 8388608
  66.3 5.2 slice-start.3
  66.3 5.2 copy-start.6
  213.2 0.7 copy-start.13
  213.2 1.3 copy-start.15
  213.9 4.1 copy-start.1
  218.1 7.4 %collective-permute-start = (bf16[2,76,768]{2,1,0:T(8,128)(2,1)S(1)}, bf16[2,76,768]{2,1,0:T(8,128)(2,1)S(1)}, u32[]{:S(2)}, u32[]{:S(2)}) collective-permute-start(bf16[2,76,768]{2,1,0:T(8,128)(2,1)S(1)} %slice.103), channel_id=1, source_target_pairs={{0,1},{1,0},{2,3},{3,2},{4,5},{5,4},{6,7},{7,6},{8,9},{9,8},{10,11... | collective-permute-start | bytes 700424 | tf_op jit(solution)/shard_map/ppermute | solution.py:19
  227.0 2.1 copy-start.10
  227.3 5.6 copy-start.8
  234.9 81.1 %copy-start.14 = (f32[384]{0:T(512)S(1)}, f32[384]{0:T(512)}, u32[]{:S(2)}) copy-start(f32[384]{0:T(512)} %param.19) | copy-start | bytes 4612
  234.9 81.7 %copy-start.16 = (f32[384]{0:T(512)S(1)}, f32[384]{0:T(512)}, u32[]{:S(2)}) copy-start(f32[384]{0:T(512)} %param.20) | copy-start | bytes 4612
  361.4 3.1 copy-start.20
  361.4 3.1 copy-start.21
  364.4 2.4 copy-start.3
  364.5 5.2 collective-permute-start.1
  370.2 1.5 copy-start.11
  370.4 4.9 slice-start
  371.6 3.7 slice-start.1
  424.8 11.1 %copy-start.18 = (f32[768]{0:T(1024)}, f32[768]{0:T(1024)S(1)}, u32[]{:S(2)}) copy-start(f32[768]{0:T(1024)S(1)} %get-tuple-element.95) | copy-start | bytes 9220
  424.8 11.1 %copy-start.19 = (f32[768]{0:T(1024)}, f32[768]{0:T(1024)S(1)}, u32[]{:S(2)}) copy-start(f32[768]{0:T(1024)S(1)} %get-tuple-element.96) | copy-start | bytes 9220
  440.9 97.2 %all-to-all-start.1 = ((bf16[2,1024,768]{2,0,1:T(2,128)(2,1)}), bf16[2,1024,768]{2,0,1:T(2,128)(2,1)}, u32[]{:S(2)}, u32[]{:S(2)}) async-start(bf16[2,1024,768]{2,0,1:T(2,128)(2,1)} %copy.86), calls=%async_computation.1 | async-start | bytes 6291456 | tf_op jit(solution)/shard_map/all_to_all | solution.py:209
  446.1 201.8 %all-reduce.5.cloned.1.call-start = ((), (), s32[]{:S(2)}) async-start(), calls=%async_computation.2 | async-start | bytes 9437184 | tf_op jit(solution)/shard_map/psum | solution.py:199
  446.2 4.3 copy-start.4
  446.2 4.3 copy-start.9
  456.2 1.9 copy-start.2
  460.5 1.4 copy-start.5
  460.5 1.7 copy-start.7
  460.5 1.7 copy-start.17
  647.9 4.1 copy-start.12
Sparse Core Ops, SparseCore 0:
  460.7 187.1 all-reduce.4
where the time goes:
time: 668 us; the launch traced here: 660 us
  blocking collectives  239 us (36%)
  waiting for transfers between devices  189 us (28%)
  local copies, waits for them, and re-layouts  88.1 us (13%)
  other arithmetic  73 us (11%)
  matrix products  38.7 us (6%)
  starting transfers between devices  17.3 us (3%)
  between operations  15.1 us (2%)
    psum x2, blocking collectives, moments(): lax.psum(jnp.sum(deviation * deviation, axis=(0, 1)), ('grp', 'seq'))  83.4 us
    psum x2, blocking collectives, moments(): lax.psum(jnp.sum(values * valid_mask, axis=(0, 1)), ('grp', 'seq'))  76 us
    all_to_all x1, waiting for transfers between devices, per_device(): lax.all_to_all(grad_pooled.astype(jnp.bfloat16), 'seq', split_axis=1, con...  68.6 us
    psum x1, waiting for transfers between devices, per_device(): lax.psum((entry_gain_part, entry_shift_part, kernel_part), ('grp', 'seq'))  57 us
    all_to_all x1, waiting for transfers between devices, per_device(): lax.all_to_all(outgoing, 'seq', split_axis=0, concat_axis=1, tiled=True)  55.5 us
    unnamed x61, local copies, waits for them, and re-layouts  43.3 us
    psum x1, blocking collectives, per_device(): lax.psum((entry_gain_part, entry_shift_part, kernel_part), ('grp', 'seq'))  41.3 us
    psum x1, blocking collectives, per_device(): lax.psum((middle_gain_part, middle_shift_part, pointwise_part, bias_part)...  38.7 us
  transfers between devices with their start and end apart: 5, of which 5 were waited for; matrix products, arithmetic and copies ran while one was open for 14% of the time, Pallas kernels for 0%

commit v1 on v0

--- a/solution.py
+++ b/solution.py
@@ -7,6 +7,20 @@
 WINDOW_SPAN = 1024
 HALF_WINDOW_ROWS = 512
 EPSILON = 0.001
+
+
+def connect_the_loops(frame_in, row_dim, load):
+    plain, out_arr = (frame_in.shape[:row_dim], frame_in.shape[row_dim + 1 :])
+    n_now = frame_in.reshape(*plain, load, -1, *out_arr)
+    return jnp.moveaxis(n_now, row_dim, 0)
+
+
+def edge_open(panel, axis_no):
+    panel = jnp.moveaxis(panel, 0, axis_no)
+    m_next = panel.shape
+    return panel.reshape(
+        *m_next[:axis_no], m_next[axis_no] * m_next[axis_no + 1], *m_next[axis_no + 2 :]
+    )
 
 
 def from_partner(block, axis, bit):
@@ -86,7 +100,20 @@
         ).reshape(-1)
     ]
     outgoing = jnp.take(pooled_low, picked, axis=0)
-    arrived = lax.all_to_all(outgoing, "seq", split_axis=0, concat_axis=1, tiled=True)
+    e_now = jax.lax.axis_index("seq")
+    built = jax.lax.axis_size("seq")
+    current_arr, r2 = (built, e_now)
+    passed = connect_the_loops(outgoing, 0, current_arr)
+    blocks_here = [passed[r2]]
+    at = 1
+    while at < current_arr:
+        part_now = passed[r2 ^ at]
+        arr_now = jax.lax.ppermute(part_now, "seq", [(jj, jj ^ at) for jj in range(current_arr)])
+        blocks_here.append(arr_now)
+        at += 1
+    state_now = jnp.stack(blocks_here)
+    passed = state_now[r2 ^ jnp.arange(current_arr)]
+    arrived = edge_open(passed, 1)
     partner_place = jnp.bitwise_xor(seq_place, 1)
     own_windows = lax.dynamic_slice_in_dim(window_order, seq_place * position_count, position_count)
     partner_windows = lax.dynamic_slice_in_dim(

time: 668 us -> 678 us (1.015)
  local copies, waits for them, and re-layouts: 88.1 us -> 105 us
  waiting for transfers between devices: 189 us -> 173 us
    all_to_all x1 -> x0, waiting for transfers between devices: 55.5 us -> none  [per_device(): lax.all_to_all(outgoing, 'seq', split_axis=0, concat_axis=1, tiled=True)]
    ppermute x0 -> x7, waiting for transfers between devices: none -> 41.2 us  [per_device(): jax.lax.ppermute(part_now, 'seq', [(jj, jj ^ at) for jj in range(current_...]
    ppermute x0 -> x7, starting transfers between devices: none -> 13.1 us  [per_device(): jax.lax.ppermute(part_now, 'seq', [(jj, jj ^ at) for jj in range(current_...]
    all_to_all x1 -> x0, starting transfers between devices: 7.41 us -> none  [per_device(): lax.all_to_all(outgoing, 'seq', split_axis=0, concat_axis=1, tiled=True)]
    unnamed x61 -> x85, local copies, waits for them, and re-layouts: 43.3 us -> 50.4 us
  transfers between devices with their start and end apart: 5 -> 11, of which waited for: 5 -> 7; matrix products, arithmetic and copies ran while one was open for 14% -> 14% of each run, Pallas kernels for 0% -> 0%
where the time goes in v1:
time: 678 us; the launch traced here: 670 us
  blocking collectives  240 us (35%)
  waiting for transfers between devices  173 us (26%)
  local copies, waits for them, and re-layouts  105 us (15%)
  other arithmetic  75.4 us (11%)
  matrix products  38.7 us (6%)
  starting transfers between devices  23.5 us (3%)
  between operations  15.2 us (2%)
    psum x2, blocking collectives, moments(): lax.psum(jnp.sum(deviation * deviation, axis=(0, 1)), ('grp', 'seq'))  83.2 us
    psum x2, blocking collectives, moments(): lax.psum(jnp.sum(values * valid_mask, axis=(0, 1)), ('grp', 'seq'))  76.3 us
    all_to_all x1, waiting for transfers between devices, per_device(): lax.all_to_all(grad_pooled.astype(jnp.bfloat16), 'seq', split_axis=1, con...  68.5 us
    psum x1, waiting for transfers between devices, per_device(): lax.psum((entry_gain_part, entry_shift_part, kernel_part), ('grp', 'seq'))  56.2 us
    unnamed x85, local copies, waits for them, and re-layouts  50.4 us
    ppermute x7, waiting for transfers between devices, per_device(): jax.lax.ppermute(part_now, 'seq', [(jj, jj ^ at) for jj in range(current_...  41.2 us
    psum x1, blocking collectives, per_device(): lax.psum((entry_gain_part, entry_shift_part, kernel_part), ('grp', 'seq'))  40.9 us
    psum x1, blocking collectives, per_device(): lax.psum((middle_gain_part, middle_shift_part, pointwise_part, bias_part)...  39.1 us
  transfers between devices with their start and end apart: 11, of which 7 were waited for; matrix products, arithmetic and copies ran while one was open for 14% of the time, Pallas kernels for 0%

profile of v1, /device:TPU:0, one launch (start us, length us, event | category | flops | bytes accessed | tf_op | source)
XLA Modules:
  0.0 670.4 jit_solution(6710531502237355332)
XLA Ops:
  9.3 16.6 %copy.79 = f32[16,256,768]{2,0,1:T(8,128)} copy(f32[16,256,768]{2,1,0:T(8,128)} %param.15) | data formatting | bytes 25165824 | tf_op args[0]
  25.9 10.5 %fusion.89 = (f32[16,128,1,768]{3,0,2,1:T(8,128)}, f32[16,128,1,768]{3,0,2,1:T(8,128)}) fusion(f32[16,128,2,768]{3,0,2,1:T(8,128)} %bitcast.200), kind=kLoop, calls=%fused_computation.189 | loop fusion | bytes 25165824 | tf_op jit(solution)/shard_map/slice | solution.py:85
  36.6 11.4 %multiply_convert_fusion.1 = (bf16[16,128,768]{2,1,0:T(8,128)(2,1)}, pred[16,128,768]{2,1,0:T(8,128)(4,1)}) fusion(f32[16,128,1,768]{3,0,2,1:T(8,128)} %get-tuple-element.66, f32[16,128,1,768]{3,0,2,1:T(8,128)} %get-tuple-element.65, f32[16,128]{1,0:T(8,128)S(1)} %compare_convert_fusion.2), kind=kLoop, calls=%fused_computation.49 | loop fusion | flops 6291456 | bytes 17309696 | tf_op jit(solution)/shard_map/convert_element_type | solution.py:92
  48.0 4.3 gather_fusion.4
  52.3 2.3 broadcast_select_fusion.1
  56.3 6.0 collective-permute-start.6
  63.3 3.4 collective-permute-start.1
  70.9 5.8 multiply_convert_fusion.2
  76.7 3.5 fusion.38
  84.7 12.7 %collective-permute-done.1 = bf16[2,128,768]{2,1,0:T(8,128)(2,1)} collective-permute-done((bf16[2,128,768]{2,1,0:T(8,128)(2,1)}, bf16[2,128,768]{2,1,0:T(8,128)(2,1)}, u32[]{:S(2)}, u32[]{:S(2)}) %collective-permute-start.1) | collective-permute-done | bytes 393248 | tf_op jit(solution)/shard_map/ppermute | solution.py:111
  100.5 5.3 collective-permute-done.2
  106.6 23.2 %collective-permute-done.3 = bf16[2,128,768]{2,1,0:T(8,128)(2,1)S(1)} collective-permute-done((bf16[2,128,768]{2,1,0:T(8,128)(2,1)S(1)}, bf16[2,128,768]{2,1,0:T(8,128)(2,1)S(1)}, u32[]{:S(2)}, u32[]{:S(2)}) %collective-permute-start.3) | collective-permute-done | bytes 393248 | tf_op jit(solution)/shard_map/ppermute | solution.py:111
  132.9 2.8 gather_fusion.1
  135.6 3.4 convert_bitcast_fusion
  139.7 37.8 %psum.77 = f32[768]{0:T(1024)S(1)} all-reduce(f32[768]{0:T(1024)S(1)} %multiply_reduce_fusion.2), channel_id=1, replica_groups=mesh['grp'=4,'seq'=8] {'grp','seq'}, use_global_device_ids=true, to_apply=%region_1.4 | all-reduce | flops 768 | bytes 6144 | tf_op jit(solution)/shard_map/psum | solution.py:41
  179.3 41.9 %psum.78 = f32[768]{0:T(1024)S(1)} all-reduce(f32[768]{0:T(1024)S(1)} %multiply_reduce_fusion.1), channel_id=1, replica_groups=mesh['grp'=4,'seq'=8] {'grp','seq'}, use_global_device_ids=true, to_apply=%region_4.7 | all-reduce | flops 768 | bytes 6144 | tf_op jit(solution)/shard_map/psum | solution.py:43
  221.2 3.5 copy.82
  225.4 3.5 multiply_convert_fusion
  228.9 2.3 collective-permute-start.7
  231.5 4.4 collective-permute-done.7
  237.7 1.9 copy-done.11
  239.6 1.8 fusion.43
  243.2 2.0 multiply_reduce_fusion.6
  245.3 38.5 %psum.79 = f32[384]{0:T(512)S(1)} all-reduce(f32[384]{0:T(512)S(1)} %get-tuple-element.94), channel_id=1, replica_groups=mesh['grp'=4,'seq'=8] {'grp','seq'}, use_global_device_ids=true, to_apply=%region_6.9 | all-reduce | flops 384 | bytes 3072 | tf_op jit(solution)/shard_map/psum | solution.py:41
  284.9 41.3 %psum.80 = f32[384]{0:T(512)S(1)} all-reduce(f32[384]{0:T(512)S(1)} %multiply_reduce_fusion.5), channel_id=1, replica_groups=mesh['grp'=4,'seq'=8] {'grp','seq'}, use_global_device_ids=true, to_apply=%region_8.11 | all-reduce | flops 384 | bytes 3072 | tf_op jit(solution)/shard_map/psum | solution.py:43
  327.0 6.1 fusion.84
  333.0 39.1 %all-reduce.1 = (f32[384]{0:T(512)S(1)}, f32[384]{0:T(512)S(1)}) all-reduce(f32[384]{0:T(512)S(1)} %get-tuple-element.50, f32[384]{0:T(512)S(1)} %get-tuple-element.49), channel_id=1, replica_groups=mesh['grp'=4,'seq'=8] {'grp','seq'}, use_global_device_ids=true, to_apply=%region_12.15 | all-reduce | flops 768 | bytes 6144 | tf_op jit(solution)/shard_map/psum | solution.py:183
  372.2 3.1 multiply_convert_fusion.5
  375.3 2.3 collective-permute-start.8
  377.8 2.7 collective-permute-done.8
  386.2 8.2 %fusion.83 = (f32[768]{0:T(1024)S(1)}, f32[768]{0:T(1024)S(1)}, f32[4,512,768]{2,1,0:T(8,128)}) fusion(f32[768]{0:T(1024)S(1)} %get-tuple-element.59, f32[4,512,768]{2,1,0:T(8,128)S(1)} %bitcast.195, f32[768]{0:T(1024)S(1)} %broadcast_divide_fusion, f32[768]{0:T(1024)S(1)} %copy-done.22, f32[768]{0:T(1024)S(1)} %copy-done.19, f32[4,512]{1,0:T(4,128)S(1)} %copy-done.18, ...), kind=kOutput, calls=%fused_computation.185 | convolution fusion | flops 1253571072 | bytes 27359232 | tf_op jit(solution)/shard_map/hrf,cf->hrc/dot_general | solution.py:215
  394.3 40.9 %all-reduce = (f32[768]{0:T(1024)S(1)}, f32[768]{0:T(1024)S(1)}, f32[768]{0:T(1024)}) all-reduce(f32[768]{0:T(1024)S(1)} %get-tuple-element.48, f32[768]{0:T(1024)S(1)} %get-tuple-element.47, f32[768]{0:T(1024)S(1)} %copy-done.21), channel_id=1, replica_groups=mesh['grp'=4,'seq'=8] {'grp','seq'}, use_global_device_ids=true, to_apply=%region_16.19 | all-reduce | flops 2304 | bytes 18432 | tf_op jit(solution)/shard_map/psum | solution.py:226
  435.2 11.1 %fusion.10 = bf16[2,1024,768]{2,1,0:T(8,128)(2,1)S(1)} fusion(f32[2,1024,768]{2,1,0:T(8,128)} %bitcast.196, f32[2,8,128,768]{3,2,1,0:T(8,128)} %copy-done.1, f32[]{:T(128)} %convert_reduce_fusion, f32[768]{0:T(1024)S(1)} %get-tuple-element.103, f32[768]{0:T(1024)S(1)} %get-tuple-element.104, f32[768]{0:T(1024)S(1)} %get-tuple-element.58, ...), kind=kLoop, calls=%fused_computation.22 | loop fusion | flops 51904512 | bytes 22049796 | tf_op jit(solution)/shard_map/convert_element_type | solution.py:237
  446.4 4.9 copy.86
  451.3 5.7 all-to-all-start
  457.0 4.3 fusion.60
  465.0 2.0 pad_maximum_fusion.2
  468.9 2.4 convolution_bitcast_fusion
  473.1 7.3 %fusion.19 = f32[2,1024,768]{2,1,0:T(8,128)} fusion(f32[2,8,128,768]{3,2,1,0:T(8,128)} %copy-done.1, f32[768]{0:T(1024)S(1)} %copy-done.24, f32[2,1024]{1,0:T(2,128)S(1)} %compare_convert_fusion.1, bf16[2,1024,384]{2,1,0:T(8,128)(2,1)S(1)} %copy-done.5, f32[384,768]{1,0:T(8,128)S(1)} %copy-done.7), kind=kOutput, calls=%fused_computation.36 | convolution fusion | flops 1212973056 | bytes 15346688 | tf_op jit(solution)/shard_map/krf,fd->krd/dot_general | solution.py:162
  480.5 68.5 %all-to-all-done = bf16[2,1024,768]{2,0,1:T(2,128)(2,1)} async-done(((bf16[2,1024,768]{2,0,1:T(2,128)(2,1)}), bf16[2,1024,768]{2,0,1:T(2,128)(2,1)}, u32[]{:S(2)}, u32[]{:S(2)}) %all-to-all-start) | async-done | bytes 3145760 | tf_op jit(solution)/shard_map/all_to_all | solution.py:236
  548.9 2.3 copy.87
  551.4 2.4 gather_fusion.5
  553.9 5.3 select_bitcast_fusion.1
  559.1 9.1 %pad_maximum_fusion = f32[16,128,2,768]{3,1,0,2:T(8,128)} fusion(f32[16,128,1,768]{3,1,0,2:T(8,128)} %get-tuple-element.70, f32[16,128,1,768]{3,1,0,2:T(8,128)S(1)} %get-tuple-element.69), kind=kLoop, calls=%fused_computation.7 | loop fusion | flops 3145728 | bytes 25165824 | tf_op jit(solution)/shard_map/stack | solution.py:246
  568.3 16.5 %copy.89 = f32[16,128,2,768]{3,0,2,1:T(8,128)} copy(f32[16,128,2,768]{3,1,0,2:T(8,128)} %pad_maximum_fusion) | data formatting | bytes 25165824 | tf_op jit(solution)/shard_map/stack | solution.py:246
  584.8 16.9 %copy.94 = f32[16,256,768]{2,1,0:T(8,128)} copy(f32[16,256,768]{2,0,1:T(8,128)} %bitcast.201) | data formatting | bytes 25165824
  601.7 56.2 %all-reduce.5.cloned.1.call-done = (f32[3,768,384]{2,1,0:T(8,128)}, f32[384,768]{1,0:T(8,128)}) async-done(((f32[3,768,384]{2,1,0:T(8,128)}, f32[384,768]{1,0:T(8,128)}), (f32[3,768,384]{2,1,0:T(8,128)}, f32[384,768]{1,0:T(8,128)})) %all-reduce.5.cloned.1.call-update) | async-done | bytes 4718608 | tf_op jit(solution)/shard_map/psum | solution.py:226
  657.9 4.1 copy.134
  (169 shorter events, 43.6 us)
Async XLA Ops:
  8.7 0.6 copy-start.29
  25.9 10.6 %copy-start.31 = (s32[64]{0:T(128)S(1)}, s32[64]{0:T(128)}, u32[]{:S(2)}) copy-start(s32[64]{0:T(128)} %param.23) | copy-start | bytes 772
  36.6 11.4 %copy-start.16 = (f32[16,128]{1,0:T(8,128)}, f32[16,128]{1,0:T(8,128)S(1)}, u32[]{:S(2)}) copy-start(f32[16,128]{1,0:T(8,128)S(1)} %compare_convert_fusion.2) | copy-start | bytes 24580
  54.6 14.3 %copy-start = (s32[1,16]{1,0:T(1,128)S(1)}, s32[1,16]{1,0:T(1,128)}, u32[]{:S(2)}) copy-start(s32[1,16]{1,0:T(1,128)} %param.24) | copy-start | bytes 196
  54.6 22.1 %slice-start.2 = ((s8[6291456]{0:T(1024)(128)(4,1)}), s8[2097152]{0:T(1024)(128)(4,1)S(1)}, s32[]{:S(2)}) async-start(s8[6291456]{0:T(1024)(128)(4,1)} %bitcast.197), calls=%async_computation.4 | async-start | bytes 4194304
  56.3 75.8 %collective-permute-start.6 = (bf16[2,128,768]{2,1,0:T(8,128)(2,1)}, bf16[2,128,768]{2,1,0:T(8,128)(2,1)S(1)}, u32[]{:S(2)}, u32[]{:S(2)}) collective-permute-start(bf16[2,128,768]{2,1,0:T(8,128)(2,1)} %get-tuple-element.74), channel_id=1, source_target_pairs={{0,7},{1,6},{2,5},{3,4},{4,3},{5,2},{6,1},{7,0},{8,15},{9,14},{10,... | collective-permute-start | bytes 1179656 | tf_op jit(solution)/shard_map/ppermute | solution.py:111
  62.3 69.0 %collective-permute-start.5 = (bf16[2,128,768]{2,1,0:T(8,128)(2,1)}, bf16[2,128,768]{2,1,0:T(8,128)(2,1)S(1)}, u32[]{:S(2)}, u32[]{:S(2)}) collective-permute-start(bf16[2,128,768]{2,1,0:T(8,128)(2,1)} %get-tuple-element.75), channel_id=1, source_target_pairs={{0,6},{1,7},{2,4},{3,5},{4,2},{5,3},{6,0},{7,1},{8,14},{9,15},{10,... | collective-permute-start | bytes 1179656 | tf_op jit(solution)/shard_map/ppermute | solution.py:111
  62.5 68.0 %collective-permute-start.4 = (bf16[2,128,768]{2,1,0:T(8,128)(2,1)}, bf16[2,128,768]{2,1,0:T(8,128)(2,1)S(1)}, u32[]{:S(2)}, u32[]{:S(2)}) collective-permute-start(bf16[2,128,768]{2,1,0:T(8,128)(2,1)} %get-tuple-element.76), channel_id=1, source_target_pairs={{0,5},{1,4},{2,7},{3,6},{4,1},{5,0},{6,3},{7,2},{8,13},{9,12},{10,... | collective-permute-start | bytes 1179656 | tf_op jit(solution)/shard_map/ppermute | solution.py:111
  63.3 34.2 %collective-permute-start.1 = (bf16[2,128,768]{2,1,0:T(8,128)(2,1)}, bf16[2,128,768]{2,1,0:T(8,128)(2,1)}, u32[]{:S(2)}, u32[]{:S(2)}) collective-permute-start(bf16[2,128,768]{2,1,0:T(8,128)(2,1)} %get-tuple-element.79), channel_id=1, source_target_pairs={{0,2},{1,3},{2,0},{3,1},{4,6},{5,7},{6,4},{7,5},{8,10},{9,11},{10,... | collective-permute-start | bytes 1179656 | tf_op jit(solution)/shard_map/ppermute | solution.py:111
  66.6 16.3 %collective-permute-start = (bf16[2,128,768]{2,1,0:T(8,128)(2,1)}, bf16[2,128,768]{2,1,0:T(8,128)(2,1)}, u32[]{:S(2)}, u32[]{:S(2)}) collective-permute-start(bf16[2,128,768]{2,1,0:T(8,128)(2,1)} %get-tuple-element.80), channel_id=1, source_target_pairs={{0,1},{1,0},{2,3},{3,2},{4,5},{5,4},{6,7},{7,6},{8,9},{9,8},{10,11... | collective-permute-start | bytes 1179656 | tf_op jit(solution)/shard_map/ppermute | solution.py:111
  70.9 5.8 slice-start.3
  70.9 5.8 copy-start.6
  76.7 4.3 copy-start.10
  80.2 2.8 copy-start.15
  80.2 17.3 %copy-start.14 = (bf16[2,128,768]{2,1,0:T(8,128)(2,1)S(1)}, bf16[2,128,768]{2,1,0:T(8,128)(2,1)}, u32[]{:S(2)}) copy-start(bf16[2,128,768]{2,1,0:T(8,128)(2,1)} %get-tuple-element.77) | copy-start | bytes 1179652
  83.0 22.8 %collective-permute-start.2 = (bf16[2,128,768]{2,1,0:T(8,128)(2,1)S(1)}, bf16[2,128,768]{2,1,0:T(8,128)(2,1)S(1)}, u32[]{:S(2)}, u32[]{:S(2)}) collective-permute-start(bf16[2,128,768]{2,1,0:T(8,128)(2,1)S(1)} %copy-done.15), channel_id=1, source_target_pairs={{0,3},{1,2},{2,1},{3,0},{4,7},{5,6},{6,5},{7,4},{8,11},{9,10},{10,... | collective-permute-start | bytes 1179656 | tf_op jit(solution)/shard_map/ppermute | solution.py:111
  97.5 32.3 %collective-permute-start.3 = (bf16[2,128,768]{2,1,0:T(8,128)(2,1)S(1)}, bf16[2,128,768]{2,1,0:T(8,128)(2,1)S(1)}, u32[]{:S(2)}, u32[]{:S(2)}) collective-permute-start(bf16[2,128,768]{2,1,0:T(8,128)(2,1)S(1)} %copy-done.14), channel_id=1, source_target_pairs={{0,4},{1,5},{2,6},{3,7},{4,0},{5,1},{6,2},{7,3},{8,12},{9,13},{10,... | collective-permute-start | bytes 1179656 | tf_op jit(solution)/shard_map/ppermute | solution.py:111
  221.2 3.5 copy-start.19
  221.2 4.2 copy-start.22
  224.7 4.2 copy-start.1
  228.9 6.9 %collective-permute-start.7 = (bf16[2,76,768]{2,1,0:T(8,128)(2,1)S(1)}, bf16[2,76,768]{2,1,0:T(8,128)(2,1)S(1)}, u32[]{:S(2)}, u32[]{:S(2)}) collective-permute-start(bf16[2,76,768]{2,1,0:T(8,128)(2,1)S(1)} %slice.105), channel_id=1, source_target_pairs={{0,1},{1,0},{2,3},{3,2},{4,5},{5,4},{6,7},{7,6},{8,9},{9,8},{10,11... | collective-permute-start | bytes 700424 | tf_op jit(solution)/shard_map/ppermute | solution.py:33
  237.4 2.1 copy-start.11
  237.7 5.6 copy-start.8
  241.4 1.8 copy-start.18
  245.3 81.0 %copy-start.20 = (f32[384]{0:T(512)S(1)}, f32[384]{0:T(512)}, u32[]{:S(2)}) copy-start(f32[384]{0:T(512)} %param.19) | copy-start | bytes 4612
  245.3 81.7 %copy-start.23 = (f32[384]{0:T(512)S(1)}, f32[384]{0:T(512)}, u32[]{:S(2)}) copy-start(f32[384]{0:T(512)} %param.20) | copy-start | bytes 4612
  372.1 3.1 copy-start.27
  372.2 3.1 copy-start.28
  375.3 2.4 copy-start.3
  375.3 5.2 collective-permute-start.8
  381.0 1.5 copy-start.12
  381.2 4.9 slice-start
  382.5 3.7 slice-start.1
  386.2 8.2 %copy-start.21 = (f32[768]{0:T(1024)S(1)}, f32[768]{0:T(1024)}, u32[]{:S(2)}) copy-start(f32[768]{0:T(1024)} %get-tuple-element.68) | copy-start | bytes 9220
  435.2 11.1 %copy-start.25 = (f32[768]{0:T(1024)}, f32[768]{0:T(1024)S(1)}, u32[]{:S(2)}) copy-start(f32[768]{0:T(1024)S(1)} %get-tuple-element.103) | copy-start | bytes 9220
  435.2 11.1 %copy-start.26 = (f32[768]{0:T(1024)}, f32[768]{0:T(1024)S(1)}, u32[]{:S(2)}) copy-start(f32[768]{0:T(1024)S(1)} %get-tuple-element.104) | copy-start | bytes 9220
  451.3 97.6 %all-to-all-start = ((bf16[2,1024,768]{2,0,1:T(2,128)(2,1)}), bf16[2,1024,768]{2,0,1:T(2,128)(2,1)}, u32[]{:S(2)}, u32[]{:S(2)}) async-start(bf16[2,1024,768]{2,0,1:T(2,128)(2,1)} %copy.86), calls=%async_computation | async-start | bytes 6291456 | tf_op jit(solution)/shard_map/all_to_all | solution.py:236
  457.0 200.9 %all-reduce.5.cloned.1.call-start = ((), (), s32[]{:S(2)}) async-start(), calls=%async_computation.1 | async-start | bytes 9437184 | tf_op jit(solution)/shard_map/psum | solution.py:226
  457.0 4.3 copy-start.4
  457.0 4.3 copy-start.9
  467.1 1.9 copy-start.2
  471.4 0.7 copy-start.30
  471.4 1.4 copy-start.5
  471.4 1.7 copy-start.7
  471.4 1.7 copy-start.24
  551.4 2.4 copy-start.17
  657.9 4.1 copy-start.13
Sparse Core Ops, SparseCore 0:
  471.5 186.3 all-reduce.4
